TPU v7x, 32 devices: a whole 2x2x4 slice. The times are simulated.
32 devices in a mesh: dp: 8 (over z, core), expert: 4 (over y, x).
Axes of the slice: x: 2, y: 2, z: 4, core: 2. Of those that a mesh axis runs over, the one named last changes fastest.
Arguments:
- tokens: bfloat16 [24576, 2048], P(('dp', 'expert')), may hold values from -6 to 6
- target: bfloat16 [24576, 2048], P(('dp', 'expert')), may hold values from -4 to 4
- route_index: int32 [8, 4, 4, 16], P('dp', None, 'expert'), may hold values from 0 to 767, as said below
- route_count: int32 [8, 4, 4], P('dp', None, 'expert'), may hold values from 1 to 16, as said below
- route_gate: float32 [8, 4, 4, 16], P('dp', None, 'expert'), may hold values from 0.1 to 1
- gate_weight: bfloat16 [2048, 4, 768], P('dp', 'expert'), may hold values from -0.125 to 0.125
- up_weight: bfloat16 [2048, 4, 768], P('dp', 'expert'), may hold values from -0.125 to 0.125
- down_weight: bfloat16 [2048, 4, 768], P('dp', 'expert'), may hold values from -0.21875 to 0.21875
Outputs:
- token_grad: bfloat16 [24576, 2048], P(('dp', 'expert'))
- gate_gradient: float32 [2048, 4, 768], P('dp', 'expert')
- up_gradient: float32 [2048, 4, 768], P('dp', 'expert')
- down_gradient: float32 [2048, 4, 768], P('dp', 'expert')
Inputs may be any that keep to these rules, and one draw needn't show every extreme that they name: `route_index`: within each list of 16 slots the indices are distinct; each names a token of the source device. `route_count`: in every group one expert has all 16 slots live from every source device; slots at or beyond the count are unused.
All inputs are finite; a program needn't handle non-finite values.
Results may differ from a plain program's by a relative error of at most 0.0059.
Values may be sent and summed in bfloat16 or wider, within the bound.
A program may use at most 128 MiB of HBM per device.

v0:
```python
import jax
import jax.numpy as jnp
from jax import lax
from jax.sharding import PartitionSpec as P


def to_owners(block):
    return lax.all_to_all(block, "expert", split_axis=0, concat_axis=1, tiled=True)


def to_sources(block):
    return lax.all_to_all(block, "expert", split_axis=1, concat_axis=0, tiled=True)


def on_device(
    tokens, target, route_index, route_count, route_gate, gate_weight, up_weight, down_weight
):
    groups = lax.axis_size("dp")
    sources = lax.axis_size("expert")
    local_index = route_index[0, :, 0, :]
    live_count = route_count[0, :, 0]
    per_source = local_index.shape[1]
    model_width = tokens.shape[1]
    usable = jnp.arange(per_source, dtype=jnp.int32)[None, :] < live_count[:, None]
    slot_weight = jnp.where(usable, route_gate[0, :, 0, :], 0.0)
    outgoing = tokens[local_index] * usable[:, :, None].astype(tokens.dtype)
    expert_rows = to_owners(outgoing)
    full_gate, full_up, full_down = (
        lax.all_gather(gate_weight, "dp", axis=0, tiled=True),
        lax.all_gather(up_weight, "dp", axis=0, tiled=True),
        lax.all_gather(down_weight, "dp", axis=0, tiled=True),
    )
    gate_pre = jnp.einsum(
        "erd,def->erf", expert_rows, full_gate, preferred_element_type=jnp.float32
    )
    up_pre = jnp.einsum("erd,def->erf", expert_rows, full_up, preferred_element_type=jnp.float32)
    sigma = jax.nn.sigmoid(gate_pre)
    active = gate_pre * sigma
    hidden = (active * up_pre).astype(jnp.bfloat16)
    expert_out = jnp.einsum(
        "erf,def->erd", hidden, full_down, preferred_element_type=jnp.float32
    ).astype(jnp.bfloat16)
    returned = to_sources(expert_out)
    flat_index = local_index.reshape(-1)
    combined = (
        jnp.zeros((tokens.shape[0], model_width), jnp.float32)
        .at[flat_index]
        .add((slot_weight[:, :, None] * returned.astype(jnp.float32)).reshape(-1, model_width))
    )
    out_grad = combined - target.astype(jnp.float32)
    slot_grad = (slot_weight[:, :, None] * out_grad[local_index]).astype(jnp.bfloat16)
    owner_grad = to_owners(slot_grad)
    hidden_grad = jnp.einsum(
        "erd,def->erf", owner_grad, full_down, preferred_element_type=jnp.float32
    )
    gate_grad = (hidden_grad * up_pre * sigma * (1.0 + gate_pre * (1.0 - sigma))).astype(
        jnp.bfloat16
    )
    up_grad = (hidden_grad * active).astype(jnp.bfloat16)
    row_grad = (
        jnp.einsum("erf,def->erd", gate_grad, full_gate, preferred_element_type=jnp.float32)
        + jnp.einsum("erf,def->erd", up_grad, full_up, preferred_element_type=jnp.float32)
    ).astype(jnp.bfloat16)
    came_back = to_sources(row_grad)
    token_grad = (
        jnp.zeros((tokens.shape[0], model_width), jnp.float32)
        .at[flat_index]
        .add(came_back.astype(jnp.float32).reshape(-1, model_width))
        .astype(jnp.bfloat16)
    )
    factor = (groups * sources * per_source) ** (-0.5)
    rows_every, grad_every = (
        lax.all_to_all(expert_rows, "dp", split_axis=2, concat_axis=1, tiled=True),
        lax.all_to_all(owner_grad, "dp", split_axis=2, concat_axis=1, tiled=True),
    )
    hidden_piece = lax.all_gather(hidden, "dp", axis=1, tiled=True)
    gate_piece = lax.all_gather(gate_grad, "dp", axis=1, tiled=True)
    up_piece = lax.all_gather(up_grad, "dp", axis=1, tiled=True)
    gate_sum = jnp.einsum(
        "erd,erf->def", rows_every, gate_piece, preferred_element_type=jnp.float32
    )
    up_sum = jnp.einsum("erd,erf->def", rows_every, up_piece, preferred_element_type=jnp.float32)
    down_sum = jnp.einsum(
        "erd,erf->def", grad_every, hidden_piece, preferred_element_type=jnp.float32
    )
    gate_gradient = gate_sum * factor
    up_gradient = up_sum * factor
    down_gradient = down_sum * factor
    return (token_grad, gate_gradient, up_gradient, down_gradient)


def solution(mesh):
    return jax.shard_map(
        on_device,
        mesh=mesh,
        in_specs=(
            P(("dp", "expert"), None),
            P(("dp", "expert"), None),
            P("dp", None, "expert", None),
            P("dp", None, "expert"),
            P("dp", None, "expert", None),
            P("dp", "expert", None),
            P("dp", "expert", None),
            P("dp", "expert", None),
        ),
        out_specs=(
            P(("dp", "expert"), None),
            P("dp", "expert", None),
            P("dp", "expert", None),
            P("dp", "expert", None),
        ),
        check_vma=False,
    )
```

profile of v0, /device:TPU:0, one launch (start us, length us, event | category | flops | bytes accessed | tf_op | source)
XLA Modules:
  0.0 305.2 jit_solution(9919206521907058066)
XLA Ops:
  7.2 0.7 all-gather.7.cloned.1.call-update
  8.0 0.7 all-gather.9.cloned.1.call-update
  8.7 0.7 all-gather.11.cloned.1.call-update
  9.4 0.7 compare_select_fusion
  10.2 0.7 gather_fusion
  11.0 0.8 broadcast_multiply_fusion
  11.8 5.2 %all-to-all-start = ((bf16[4,16,2048]{2,1,0:T(8,128)(2,1)}), bf16[4,16,2048]{2,1,0:T(8,128)(2,1)S(1)}, u32[]{:S(2)}, u32[]{:S(2)}) async-start(bf16[4,16,2048]{2,1,0:T(8,128)(2,1)} %broadcast_multiply_fusion), calls=%async_computation | async-start | bytes 524288 | tf_op jit(solution)/shard_map/all_to_all | solution.py:8
  17.0 0.5 broadcast.132
  17.5 0.7 reduce.6
  18.3 4.1 %all-to-all-done = bf16[4,16,2048]{2,1,0:T(8,128)(2,1)S(1)} async-done(((bf16[4,16,2048]{2,1,0:T(8,128)(2,1)}), bf16[4,16,2048]{2,1,0:T(8,128)(2,1)S(1)}, u32[]{:S(2)}, u32[]{:S(2)}) %all-to-all-start) | async-done | bytes 262176 | tf_op jit(solution)/shard_map/all_to_all | solution.py:8
  22.4 1.9 copy.40
  24.3 0.5 broadcast.134
  24.9 13.3 %reduce.10 = bf16[2048,64]{1,0:T(8,128)(2,1)} reduce(bf16[2048,1,64]{2,1,0:T(2,128)(2,1)} %bitcast.114, bf16[]{:T(256)} %broadcast.134), dimensions={1}, to_apply=%bitcast.86.reduce_sub_computation | reduce | bytes 524290
  38.2 2.1 reshape.301
  40.3 4.9 %all-to-all-start.4 = ((bf16[8,2,8192]{2,1,0:T(2,128)(2,1)}), bf16[8,2,8192]{2,1,0:T(2,128)(2,1)}, u32[]{:S(2)}, u32[]{:S(2)}) async-start(bf16[8,2,8192]{2,1,0:T(2,128)(2,1)} %reshape.301), calls=%async_computation.4 | async-start | bytes 524288 | tf_op jit(solution)/shard_map/all_to_all | solution.py:73
  45.2 0.1 lt.53
  45.3 0.5 broadcast.133
  45.8 0.7 reduce.7
  46.6 8.4 %all-to-all-done.4 = bf16[8,2,8192]{2,1,0:T(2,128)(2,1)} async-done(((bf16[8,2,8192]{2,1,0:T(2,128)(2,1)}), bf16[8,2,8192]{2,1,0:T(2,128)(2,1)}, u32[]{:S(2)}, u32[]{:S(2)}) %all-to-all-start.4) | async-done | bytes 262176 | tf_op jit(solution)/shard_map/all_to_all | solution.py:73
  55.0 3.4 %reshape.302 = bf16[2048,1,64]{2,1,0:T(2,128)(2,1)} reshape(bf16[8,2,8192]{2,1,0:T(2,128)(2,1)} %all-to-all-done.4) | data formatting | bytes 524288
  58.4 3.4 %copy.41 = bf16[1,64,2048]{2,1,0:T(8,128)(2,1)} copy(bf16[1,64,2048]{1,0,2:T(2,128)(2,1)} %bitcast.112) | data formatting | bytes 524288 | tf_op jit(solution)/shard_map/all_to_all | solution.py:73
  61.8 1.7 copy.49
  63.5 3.2 %fusion.10 = f32[64,768]{1,0:T(8,128)} fusion(bf16[64,2048]{1,0:T(8,128)(2,1)S(1)} %bitcast.117, bf16[2048,1,768]{2,0,1:T(8,128)(2,1)} %all-gather.7.cloned.1.call-done), kind=kOutput, calls=%fused_computation.15 | convolution fusion | flops 201326592 | bytes 3604480 | tf_op jit(solution)/shard_map/erd,def->erf/dot_general | solution.py:33
  66.8 24.2 %all-gather.9.cloned.1.call-done = bf16[2048,1,768]{2,0,1:T(8,128)(2,1)} async-done(((bf16[256,1,768]{2,0,1:T(8,128)(2,1)}), bf16[2048,1,768]{2,0,1:T(8,128)(2,1)}) %all-gather.9.cloned.1.call-update) | async-done | bytes 3145744 | tf_op jit(solution)/shard_map/all_gather | solution.py:30
  90.9 3.2 %multiply_convert_fusion.3 = (bf16[64,768]{1,0:T(8,128)(2,1)S(1)}, f32[64,768]{1,0:T(8,128)}) fusion(f32[64,768]{1,0:T(8,128)} %fusion.10, bf16[64,2048]{1,0:T(8,128)(2,1)S(1)} %bitcast.118, bf16[2048,1,768]{2,0,1:T(8,128)(2,1)} %all-gather.9.cloned.1.call-done), kind=kOutput, calls=%fused_computation.44 | convolution fusion | flops 201621504 | bytes 3899392 | tf_op jit(solution)/shard_map/erd,def->erf/dot_general | solution.py:36
  94.1 35.6 %all-gather.11.cloned.1.call-done = bf16[2048,1,768]{2,0,1:T(8,128)(2,1)} async-done(((bf16[256,1,768]{2,0,1:T(8,128)(2,1)}), bf16[2048,1,768]{2,0,1:T(8,128)(2,1)}) %all-gather.11.cloned.1.call-update) | async-done | bytes 3145744 | tf_op jit(solution)/shard_map/all_gather | solution.py:31
  129.7 3.0 fusion.25
  132.7 1.2 copy.62
  133.9 3.8 %reduce.8 = bf16[64,2048]{1,0:T(8,128)(2,1)} reduce(bf16[64,1,2048]{2,1,0:T(2,128)(2,1)} %bitcast.123, bf16[]{:T(256)} %broadcast.134), dimensions={1}, to_apply=%bitcast.109.reduce_sub_computation | reduce | bytes 524290
  137.7 1.8 reshape.297
  139.5 4.2 %all-to-all-start.1 = ((bf16[4,2,16384]{2,1,0:T(2,128)(2,1)}), bf16[4,2,16384]{2,1,0:T(2,128)(2,1)}, u32[]{:S(2)}, u32[]{:S(2)}) async-start(bf16[4,2,16384]{2,1,0:T(2,128)(2,1)} %reshape.297), calls=%async_computation.1 | async-start | bytes 524288 | tf_op jit(solution)/shard_map/all_to_all | solution.py:12
  143.8 5.8 %all-to-all-done.1 = bf16[4,2,16384]{2,1,0:T(2,128)(2,1)} async-done(((bf16[4,2,16384]{2,1,0:T(2,128)(2,1)}), bf16[4,2,16384]{2,1,0:T(2,128)(2,1)}, u32[]{:S(2)}, u32[]{:S(2)}) %all-to-all-start.1) | async-done | bytes 262176 | tf_op jit(solution)/shard_map/all_to_all | solution.py:12
  149.7 1.9 reshape.298
  151.5 5.1 %scatter_custom_fusion = f32[768,2048]{1,0:T(8,128)} fusion(s32[64]{0:T(128)S(1)} %fusion.41, f32[]{:T(128)} %constant.5.clone.1, bf16[1,64,2048]{2,0,1:T(2,128)(2,1)} %bitcast.122, f32[64]{0:T(128)S(1)} %broadcast_select_fusion.1), kind=kCustom, calls=%fused_computation.19 | custom fusion | flops 393216 | bytes 6554116 | tf_op jit(solution)/shard_map/scatter-add | solution.py:48
  156.6 7.9 %convert_subtract_fusion = f32[768,2048]{1,0:T(8,128)} fusion(f32[768,2048]{1,0:T(8,128)} %scatter_custom_fusion, bf16[768,2048]{1,0:T(8,128)(2,1)} %param.9), kind=kLoop, calls=%fused_computation.4 | loop fusion | flops 3145728 | bytes 15728640 | tf_op jit(solution)/shard_map/sub | solution.py:50
  164.4 4.6 %gather_fusion.1 = f32[64,2048]{1,0:T(8,128)} fusion(f32[768,2048]{1,0:T(8,128)} %convert_subtract_fusion, s32[1024]{0:T(1024)S(1)} %pad_clamp_fusion), kind=kCustom, calls=%fused_computation.1 | custom fusion | bytes 1048832 | tf_op jit(solution)/shard_map/gather | solution.py:51
  169.0 1.8 multiply_convert_fusion
  170.8 4.1 %all-to-all-start.2 = ((bf16[4,16,2048]{2,1,0:T(8,128)(2,1)}), bf16[4,16,2048]{2,1,0:T(8,128)(2,1)}, u32[]{:S(2)}, u32[]{:S(2)}) async-start(bf16[4,16,2048]{2,1,0:T(8,128)(2,1)} %multiply_convert_fusion), calls=%async_computation.2 | async-start | bytes 524288 | tf_op jit(solution)/shard_map/all_to_all | solution.py:8
  174.9 16.5 %all-gather.2 = bf16[512,768]{1,0:T(8,128)(2,1)} all-gather(bf16[64,768]{1,0:T(8,128)(2,1)S(1)} %get-tuple-element.28), channel_id=4, replica_groups=mesh['dp'=8,'expert'=4] {'dp'}, dimensions={0}, use_global_device_ids=true | all-gather | bytes 884736 | tf_op jit(solution)/shard_map/all_gather | solution.py:76
  191.4 2.8 multiply_convert_fusion.2
  194.2 0.2 copy-done.2
  194.4 1.1 fusion.4
  195.5 1.1 fusion.28
  196.5 1.2 copy.61
  197.7 3.8 %reduce.9 = bf16[64,2048]{1,0:T(8,128)(2,1)} reduce(bf16[64,1,2048]{2,1,0:T(2,128)(2,1)} %bitcast.124, bf16[]{:T(256)} %broadcast.134), dimensions={1}, to_apply=%bitcast.108.reduce_sub_computation | reduce | bytes 524290
  201.5 1.9 reshape.299
  203.4 4.2 %all-to-all-start.3 = ((bf16[4,2,16384]{2,1,0:T(2,128)(2,1)}), bf16[4,2,16384]{2,1,0:T(2,128)(2,1)}, u32[]{:S(2)}, u32[]{:S(2)}) async-start(bf16[4,2,16384]{2,1,0:T(2,128)(2,1)} %reshape.299), calls=%async_computation.3 | async-start | bytes 524288 | tf_op jit(solution)/shard_map/all_to_all | solution.py:12
  207.6 16.5 %all-gather = bf16[512,768]{1,0:T(8,128)(2,1)S(1)} all-gather(bf16[64,768]{1,0:T(8,128)(2,1)} %copy-done.4), channel_id=2, replica_groups=mesh['dp'=8,'expert'=4] {'dp'}, dimensions={0}, use_global_device_ids=true | all-gather | bytes 884736 | tf_op jit(solution)/shard_map/all_gather | solution.py:77
  224.1 1.3 fusion.33
  225.4 3.0 copy.46
  228.4 3.4 %copy.43 = bf16[1,64,2048]{1,0,2:T(2,128)(2,1)} copy(bf16[1,64,2048]{2,1,0:T(8,128)(2,1)} %bitcast.22) | data formatting | bytes 524288 | tf_op jit(solution)/shard_map/all_to_all | solution.py:8
  231.8 13.3 %reduce.11 = bf16[2048,64]{1,0:T(8,128)(2,1)} reduce(bf16[2048,1,64]{2,1,0:T(2,128)(2,1)} %bitcast.115, bf16[]{:T(256)} %broadcast.134), dimensions={1}, to_apply=%bitcast.88.reduce_sub_computation | reduce | bytes 524290
  245.1 2.1 reshape.303
  247.3 4.1 %all-to-all-start.5 = ((bf16[8,2,8192]{2,1,0:T(2,128)(2,1)}), bf16[8,2,8192]{2,1,0:T(2,128)(2,1)}, u32[]{:S(2)}, u32[]{:S(2)}) async-start(bf16[8,2,8192]{2,1,0:T(2,128)(2,1)} %reshape.303), calls=%async_computation.5 | async-start | bytes 524288 | tf_op jit(solution)/shard_map/all_to_all | solution.py:74
  251.3 19.9 %all-gather.1 = bf16[512,768]{1,0:T(8,128)(2,1)S(1)} all-gather(bf16[64,768]{1,0:T(8,128)(2,1)S(1)} %get-tuple-element.25), channel_id=3, replica_groups=mesh['dp'=8,'expert'=4] {'dp'}, dimensions={0}, use_global_device_ids=true | all-gather | bytes 884736 | tf_op jit(solution)/shard_map/all_gather | solution.py:78
  271.3 1.3 fusion.32
  272.6 3.0 copy.47
  275.6 1.9 reshape.300
  277.5 5.1 %scatter_custom_fusion.1 = f32[768,2048]{1,0:T(8,128)} fusion(s32[64]{0:T(128)S(1)} %fusion.41, f32[]{:T(128)} %constant.5.clone.1, bf16[1,64,2048]{2,0,1:T(2,128)(2,1)} %bitcast.125), kind=kCustom, calls=%fused_computation.17 | custom fusion | flops 262144 | bytes 6553604 | tf_op jit(solution)/shard_map/scatter-add | solution.py:68
  282.5 4.9 %convert_element_type.75 = bf16[768,2048]{1,0:T(8,128)(2,1)} convert(f32[768,2048]{1,0:T(8,128)} %scatter_custom_fusion.1) | non-fusion elementwise | flops 1572864 | bytes 9437184 | tf_op jit(solution)/shard_map/convert_element_type | solution.py:69
  287.5 3.4 %reshape.304 = bf16[2048,1,64]{2,1,0:T(2,128)(2,1)} reshape(bf16[8,2,8192]{2,1,0:T(2,128)(2,1)} %all-to-all-done.5) | data formatting | bytes 524288
  290.8 2.3 copy.44
  293.3 2.4 fusion.31
  295.7 3.0 copy.48
  (35 shorter events, 0.8 us)
Async XLA Ops:
  7.2 3.0 copy-start
  7.2 10.4 %copy-start.5 = (s32[1,4,1,16]{3,2,1,0:T(1,128)S(1)}, s32[1,4,1,16]{3,2,1,0:T(1,128)}, u32[]{:S(2)}) copy-start(s32[1,4,1,16]{3,2,1,0:T(1,128)} %param.10) | copy-start | bytes 772
  7.2 3.8 %copy-start.7 = (s32[1,4,1]{1,2,0:T(1,128)S(1)}, s32[1,4,1]{1,2,0:T(1,128)}, u32[]{:S(2)}) copy-start(s32[1,4,1]{1,2,0:T(1,128)} %param.11) | copy-start | bytes 52
  7.2 56.3 %all-gather.7.cloned.1.call-start = ((), (), s32[]{:S(2)}) async-start(), calls=%async_computation.6 | async-start | bytes 3538944 | tf_op jit(solution)/shard_map/all_gather | solution.py:29
  7.9 83.0 %all-gather.9.cloned.1.call-start = ((), (), s32[]{:S(2)}) async-start(), calls=%async_computation.7 | async-start | bytes 3538944 | tf_op jit(solution)/shard_map/all_gather | solution.py:30
  8.7 121.0 %all-gather.11.cloned.1.call-start = ((), (), s32[]{:S(2)}) async-start(), calls=%async_computation.8 | async-start | bytes 3538944 | tf_op jit(solution)/shard_map/all_gather | solution.py:31
  10.9 34.9 %copy-start.6 = (f32[1,4,1,16]{3,2,1,0:T(1,128)S(1)}, f32[1,4,1,16]{3,2,1,0:T(1,128)}, u32[]{:S(2)}) copy-start(f32[1,4,1,16]{3,2,1,0:T(1,128)} %param.12) | copy-start | bytes 772
  11.8 10.6 %all-to-all-start = ((bf16[4,16,2048]{2,1,0:T(8,128)(2,1)}), bf16[4,16,2048]{2,1,0:T(8,128)(2,1)S(1)}, u32[]{:S(2)}, u32[]{:S(2)}) async-start(bf16[4,16,2048]{2,1,0:T(8,128)(2,1)} %broadcast_multiply_fusion), calls=%async_computation | async-start | bytes 524288 | tf_op jit(solution)/shard_map/all_to_all | solution.py:8
  40.3 14.7 %all-to-all-start.4 = ((bf16[8,2,8192]{2,1,0:T(2,128)(2,1)}), bf16[8,2,8192]{2,1,0:T(2,128)(2,1)}, u32[]{:S(2)}, u32[]{:S(2)}) async-start(bf16[8,2,8192]{2,1,0:T(2,128)(2,1)} %reshape.301), calls=%async_computation.4 | async-start | bytes 524288 | tf_op jit(solution)/shard_map/all_to_all | solution.py:73
  94.1 49.6 %copy-start.3 = (bf16[8,8,8,256]{3,2,1,0:T(8,128)(2,1)S(1)}, bf16[8,8,8,256]{3,2,1,0:T(8,128)(2,1)}, u32[]{:S(2)}) copy-start(bf16[8,8,8,256]{3,2,1,0:T(8,128)(2,1)} %copy.49) | copy-start | bytes 786436
  139.5 10.2 %all-to-all-start.1 = ((bf16[4,2,16384]{2,1,0:T(2,128)(2,1)}), bf16[4,2,16384]{2,1,0:T(2,128)(2,1)}, u32[]{:S(2)}, u32[]{:S(2)}) async-start(bf16[4,2,16384]{2,1,0:T(2,128)(2,1)} %reshape.297), calls=%async_computation.1 | async-start | bytes 524288 | tf_op jit(solution)/shard_map/all_to_all | solution.py:12
  170.8 20.5 %all-to-all-start.2 = ((bf16[4,16,2048]{2,1,0:T(8,128)(2,1)}), bf16[4,16,2048]{2,1,0:T(8,128)(2,1)}, u32[]{:S(2)}, u32[]{:S(2)}) async-start(bf16[4,16,2048]{2,1,0:T(8,128)(2,1)} %multiply_convert_fusion), calls=%async_computation.2 | async-start | bytes 524288 | tf_op jit(solution)/shard_map/all_to_all | solution.py:8
  191.4 3.0 copy-start.2
  191.4 4.1 %copy-start.1 = (bf16[2048,1,768]{2,0,1:T(8,128)(2,1)S(1)}, bf16[2048,1,768]{2,0,1:T(8,128)(2,1)}, u32[]{:S(2)}) copy-start(bf16[2048,1,768]{2,0,1:T(8,128)(2,1)} %all-gather.7.cloned.1.call-done) | copy-start | bytes 9437188
  194.2 2.3 copy-start.4
  203.4 43.9 %all-to-all-start.3 = ((bf16[4,2,16384]{2,1,0:T(2,128)(2,1)}), bf16[4,2,16384]{2,1,0:T(2,128)(2,1)}, u32[]{:S(2)}, u32[]{:S(2)}) async-start(bf16[4,2,16384]{2,1,0:T(2,128)(2,1)} %reshape.299), calls=%async_computation.3 | async-start | bytes 524288 | tf_op jit(solution)/shard_map/all_to_all | solution.py:12
  247.3 40.2 %all-to-all-start.5 = ((bf16[8,2,8192]{2,1,0:T(2,128)(2,1)}), bf16[8,2,8192]{2,1,0:T(2,128)(2,1)}, u32[]{:S(2)}, u32[]{:S(2)}) async-start(bf16[8,2,8192]{2,1,0:T(2,128)(2,1)} %reshape.303), calls=%async_computation.5 | async-start | bytes 524288 | tf_op jit(solution)/shard_map/all_to_all | solution.py:74
Sparse Core Ops, SparseCore 0:
  9.6 40.9 all-gather.6
  52.3 38.6 all-gather.8
  92.6 37.1 all-gather.10
where the time goes:
time: 307 us; the launch traced here: 305 us
  waiting for transfers between devices  80.1 us (26%)
  other arithmetic  62 us (20%)
  blocking collectives  52.9 us (17%)
  local copies, waits for them, and re-layouts  50.3 us (16%)
  starting transfers between devices  26.7 us (9%)
  matrix products  19.3 us (6%)
  between operations  13.9 us (5%)
    all_gather x1, waiting for transfers between devices, on_device(): lax.all_gather(down_weight, 'dp', axis=0, tiled=True)  35.6 us
    unnamed x6, other arithmetic  35.6 us
    unnamed x32, local copies, waits for them, and re-layouts  31.1 us
    all_gather x1, waiting for transfers between devices, on_device(): lax.all_gather(up_weight, 'dp', axis=0, tiled=True)  24.2 us
    all_gather x1, blocking collectives, on_device(): up_piece = lax.all_gather(up_grad, 'dp', axis=1, tiled=True)  19.9 us
    all_gather x1, blocking collectives, on_device(): gate_piece = lax.all_gather(gate_grad, 'dp', axis=1, tiled=True)  16.5 us
    all_gather x1, blocking collectives, on_device(): hidden_piece = lax.all_gather(hidden, 'dp', axis=1, tiled=True)  16.5 us
    all_to_all x2, starting transfers between devices, to_owners(): lax.all_to_all(block, 'expert', split_axis=0, concat_axis=1, tiled=True)  9.24 us
  transfers between devices with their start and end apart: 9, of which 5 were waited for; matrix products, arithmetic and copies ran while one was open for 25% of the time, Pallas kernels for 0%

commit v1 on v0

--- a/solution.py
+++ b/solution.py
@@ -2,6 +2,18 @@
 import jax.numpy as jnp
 from jax import lax
 from jax.sharding import PartitionSpec as P
+
+
+def summed_around(x, axis, dim, term):
+    size, place, span = (lax.axis_size(axis), lax.axis_index(axis), x.shape[dim])
+    upward = [(i, (i + 1) % size) for i in range(size)]
+    held, total = (x, None)
+    for step in range(size):
+        arriving = lax.ppermute(held, axis, upward) if step < size - 1 else None
+        update = term(held, (place - step) % size * span)
+        total = update if total is None else total + update
+        held = arriving
+    return total
 
 
 def to_owners(block):
@@ -73,15 +85,22 @@
         lax.all_to_all(expert_rows, "dp", split_axis=2, concat_axis=1, tiled=True),
         lax.all_to_all(owner_grad, "dp", split_axis=2, concat_axis=1, tiled=True),
     )
-    hidden_piece = lax.all_gather(hidden, "dp", axis=1, tiled=True)
     gate_piece = lax.all_gather(gate_grad, "dp", axis=1, tiled=True)
     up_piece = lax.all_gather(up_grad, "dp", axis=1, tiled=True)
     gate_sum = jnp.einsum(
         "erd,erf->def", rows_every, gate_piece, preferred_element_type=jnp.float32
     )
     up_sum = jnp.einsum("erd,erf->def", rows_every, up_piece, preferred_element_type=jnp.float32)
-    down_sum = jnp.einsum(
-        "erd,erf->def", grad_every, hidden_piece, preferred_element_type=jnp.float32
+    down_sum = summed_around(
+        hidden,
+        "dp",
+        1,
+        lambda part, offset: jnp.einsum(
+            "erd,erf->def",
+            lax.dynamic_slice_in_dim(grad_every, offset, part.shape[1], axis=1),
+            part,
+            preferred_element_type=jnp.float32,
+        ),
     )
     gate_gradient = gate_sum * factor
     up_gradient = up_sum * factor

time: 307 us -> 284 us (0.925)
  local copies, waits for them, and re-layouts: 50.3 us -> 25.3 us
  waiting for transfers between devices: 80.1 us -> 105 us
  blocking collectives: 52.9 us -> 35.4 us
  other arithmetic: 62 us -> 53 us
  matrix products: 19.3 us -> 24.2 us
    all_gather x1 -> x0, blocking collectives: 16.5 us -> none  [on_device(): hidden_piece = lax.all_gather(hidden, 'dp', axis=1, tiled=True)]
    unnamed x32 -> x46, local copies, waits for them, and re-layouts: 31.1 us -> 15.4 us
    all_gather x1, waiting for transfers between devices: 24.2 us -> 37.9 us  [on_device(): lax.all_gather(up_weight, 'dp', axis=0, tiled=True)]
    all_gather x1, waiting for transfers between devices: 0.01 us -> 12.8 us  [on_device(): lax.all_gather(gate_weight, 'dp', axis=0, tiled=True)]
    ppermute x0 -> x7, waiting for transfers between devices: none -> 10.4 us  [summed_around(): arriving = lax.ppermute(held, axis, upward) if step < size - 1 else None]
    all_to_all x1, waiting for transfers between devices: 8.38 us -> 0.01 us  [on_device(): lax.all_to_all(expert_rows, 'dp', split_axis=2, concat_axis=1, tiled=True)]
    unnamed x6, other arithmetic: 35.6 us -> 28.9 us
    dot_general x1 -> x8, matrix products: 2.43 us -> 7.85 us  [on_device(): jnp.einsum('erd,erf->def', lax.dynamic_slice_in_dim(grad_every, offset, p...]
  transfers between devices with their start and end apart: 9 -> 16, of which waited for: 5 -> 8; matrix products, arithmetic and copies ran while one was open for 25% -> 34% of each run, Pallas kernels for 0% -> 0%
where the time goes in v1:
time: 284 us; the launch traced here: 283 us
  waiting for transfers between devices  105 us (37%)
  other arithmetic  53 us (19%)
  blocking collectives  35.4 us (12%)
  starting transfers between devices  25.4 us (9%)
  local copies, waits for them, and re-layouts  25.3 us (9%)
  matrix products  24.2 us (9%)
  between operations  14.2 us (5%)
    all_gather x1, waiting for transfers between devices, on_device(): lax.all_gather(up_weight, 'dp', axis=0, tiled=True)  37.9 us
    all_gather x1, waiting for transfers between devices, on_device(): lax.all_gather(down_weight, 'dp', axis=0, tiled=True)  35.6 us
    unnamed x6, other arithmetic  28.9 us
    all_gather x1, blocking collectives, on_device(): up_piece = lax.all_gather(up_grad, 'dp', axis=1, tiled=True)  20 us
    all_gather x1, blocking collectives, on_device(): gate_piece = lax.all_gather(gate_grad, 'dp', axis=1, tiled=True)  15.4 us
    unnamed x46, local copies, waits for them, and re-layouts  15.4 us
    all_gather x1, waiting for transfers between devices, on_device(): lax.all_gather(gate_weight, 'dp', axis=0, tiled=True)  12.8 us
    ppermute x7, waiting for transfers between devices, summed_around(): arriving = lax.ppermute(held, axis, upward) if step < size - 1 else None  10.4 us
  transfers between devices with their start and end apart: 16, of which 8 were waited for; matrix products, arithmetic and copies ran while one was open for 34% of the time, Pallas kernels for 0%

profile of v1, /device:TPU:0, one launch (start us, length us, event | category | flops | bytes accessed | tf_op | source)
XLA Modules:
  0.0 283.0 jit_solution(1251254520554583286)
XLA Ops:
  7.3 0.7 all-gather.6.cloned.1.call-update
  8.0 0.7 all-gather.8.cloned.1.call-update
  8.7 0.7 all-gather.10.cloned.1.call-update
  9.4 0.7 compare_select_fusion
  10.2 0.7 gather_fusion
  11.0 0.8 broadcast_multiply_fusion
  11.8 5.2 %all-to-all-start = ((bf16[4,16,2048]{2,1,0:T(8,128)(2,1)}), bf16[4,16,2048]{2,1,0:T(8,128)(2,1)S(1)}, u32[]{:S(2)}, u32[]{:S(2)}) async-start(bf16[4,16,2048]{2,1,0:T(8,128)(2,1)} %broadcast_multiply_fusion), calls=%async_computation | async-start | bytes 524288 | tf_op jit(solution)/shard_map/all_to_all | solution.py:20
  17.0 0.5 broadcast.144
  17.5 0.7 reduce.6
  18.4 0.5 broadcast.145
  18.9 0.7 reduce.7
  19.7 2.7 all-to-all-done
  22.4 0.7 copy.40
  23.1 0.6 broadcast.146
  23.7 11.6 %reduce.10 = bf16[2048,64]{1,0:T(8,128)(2,1)S(1)} reduce(bf16[2048,1,64]{2,1,0:T(2,128)(2,1)S(1)} %bitcast.159, bf16[]{:T(256)} %broadcast.146), dimensions={1}, to_apply=%bitcast.132.reduce_sub_computation | reduce | bytes 524290
  35.3 1.1 reshape.366
  36.4 4.9 %all-to-all-start.4 = ((bf16[8,2,8192]{2,1,0:T(2,128)(2,1)}), bf16[8,2,8192]{2,1,0:T(2,128)(2,1)S(1)}, u32[]{:S(2)}, u32[]{:S(2)}) async-start(bf16[8,2,8192]{2,1,0:T(2,128)(2,1)} %reshape.366), calls=%async_computation.4 | async-start | bytes 524288 | tf_op jit(solution)/shard_map/all_to_all | solution.py:85
  41.3 12.8 %all-gather.6.cloned.1.call-done = bf16[2048,1,768]{2,0,1:T(8,128)(2,1)} async-done(((bf16[256,1,768]{2,0,1:T(8,128)(2,1)}), bf16[2048,1,768]{2,0,1:T(8,128)(2,1)}) %all-gather.6.cloned.1.call-update) | async-done | bytes 3145744 | tf_op jit(solution)/shard_map/all_gather | solution.py:41
  54.1 2.5 fusion.10
  56.6 37.9 %all-gather.8.cloned.1.call-done = bf16[2048,1,768]{2,0,1:T(8,128)(2,1)} async-done(((bf16[256,1,768]{2,0,1:T(8,128)(2,1)}), bf16[2048,1,768]{2,0,1:T(8,128)(2,1)}) %all-gather.8.cloned.1.call-update) | async-done | bytes 3145744 | tf_op jit(solution)/shard_map/all_gather | solution.py:42
  94.5 3.2 %multiply_convert_fusion.3 = (bf16[64,768]{1,0:T(8,128)(2,1)S(1)}, f32[64,768]{1,0:T(8,128)}) fusion(f32[64,768]{1,0:T(8,128)S(1)} %fusion.10, bf16[64,2048]{1,0:T(8,128)(2,1)S(1)} %bitcast.163, bf16[2048,1,768]{2,0,1:T(8,128)(2,1)} %all-gather.8.cloned.1.call-done), kind=kOutput, calls=%fused_computation.51 | convolution fusion | flops 201621504 | bytes 3899392 | tf_op jit(solution)/shard_map/erd,def->erf/dot_general | solution.py:48
  97.7 35.6 %all-gather.10.cloned.1.call-done = bf16[2048,1,768]{2,0,1:T(8,128)(2,1)} async-done(((bf16[256,1,768]{2,0,1:T(8,128)(2,1)}), bf16[2048,1,768]{2,0,1:T(8,128)(2,1)}) %all-gather.10.cloned.1.call-update) | async-done | bytes 3145744 | tf_op jit(solution)/shard_map/all_gather | solution.py:43
  133.3 2.9 %fusion.25 = bf16[1,64,2048]{2,1,0:T(8,128)(2,1)S(1)} fusion(bf16[64,768]{1,0:T(8,128)(2,1)S(1)} %get-tuple-element.28, bf16[2048,1,768]{2,0,1:T(8,128)(2,1)} %all-gather.10.cloned.1.call-done), kind=kOutput, calls=%fused_computation.24 | convolution fusion | flops 201457664 | bytes 3506176 | tf_op jit(solution)/shard_map/erf,def->erd/dot_general | solution.py:52
  136.7 2.2 reduce.8
  138.9 0.9 reshape.362
  140.0 3.6 %all-to-all-start.1 = ((bf16[4,2,16384]{2,1,0:T(2,128)(2,1)}), bf16[4,2,16384]{2,1,0:T(2,128)(2,1)S(1)}, u32[]{:S(2)}, u32[]{:S(2)}) async-start(bf16[4,2,16384]{2,1,0:T(2,128)(2,1)} %reshape.362), calls=%async_computation.1 | async-start | bytes 524288 | tf_op jit(solution)/shard_map/all_to_all | solution.py:24
  143.6 0.6 reshape.367
  144.3 0.6 copy.41
  144.9 0.8 collective-permute-done
  145.7 4.0 %all-to-all-done.1 = bf16[4,2,16384]{2,1,0:T(2,128)(2,1)S(1)} async-done(((bf16[4,2,16384]{2,1,0:T(2,128)(2,1)}), bf16[4,2,16384]{2,1,0:T(2,128)(2,1)S(1)}, u32[]{:S(2)}, u32[]{:S(2)}) %all-to-all-start.1) | async-done | bytes 262176 | tf_op jit(solution)/shard_map/all_to_all | solution.py:24
  149.7 1.0 reshape.363
  150.7 5.3 %scatter_custom_fusion = f32[768,2048]{1,0:T(8,128)} fusion(s32[64]{0:T(128)S(1)} %fusion.74, f32[]{:T(128)} %constant.67.clone.1, bf16[1,64,2048]{2,0,1:T(2,128)(2,1)} %bitcast.169, f32[64]{0:T(128)S(1)} %broadcast_select_fusion.1), kind=kCustom, calls=%fused_computation.19 | custom fusion | flops 393216 | bytes 6554116 | tf_op jit(solution)/shard_map/scatter-add | solution.py:60
  155.9 6.9 %convert_subtract_fusion = f32[768,2048]{1,0:T(8,128)} fusion(f32[768,2048]{1,0:T(8,128)} %scatter_custom_fusion, bf16[768,2048]{1,0:T(8,128)(2,1)S(1)} %copy-done.3), kind=kLoop, calls=%fused_computation.4 | loop fusion | flops 3145728 | bytes 15728640 | tf_op jit(solution)/shard_map/sub | solution.py:62
  162.8 3.8 %gather_fusion.1 = f32[64,2048]{1,0:T(8,128)S(1)} fusion(f32[768,2048]{1,0:T(8,128)} %convert_subtract_fusion, s32[1024]{0:T(1024)S(1)} %pad_clamp_fusion), kind=kCustom, calls=%fused_computation.1 | custom fusion | bytes 1048832 | tf_op jit(solution)/shard_map/gather | solution.py:63
  166.6 0.8 multiply_convert_fusion
  167.4 3.4 %all-to-all-start.2 = ((bf16[4,16,2048]{2,1,0:T(8,128)(2,1)}), bf16[4,16,2048]{2,1,0:T(8,128)(2,1)S(1)}, u32[]{:S(2)}, u32[]{:S(2)}) async-start(bf16[4,16,2048]{2,1,0:T(8,128)(2,1)} %multiply_convert_fusion), calls=%async_computation.2 | async-start | bytes 524288 | tf_op jit(solution)/shard_map/all_to_all | solution.py:20
  171.0 6.1 %collective-permute-done.2 = bf16[1,64,768]{2,1,0:T(8,128)(2,1)} collective-permute-done((bf16[1,64,768]{2,1,0:T(8,128)(2,1)}, bf16[1,64,768]{2,1,0:T(8,128)(2,1)}, u32[]{:S(2)}, u32[]{:S(2)}) %collective-permute-start.2) | collective-permute-done | bytes 98336 | tf_op jit(solution)/shard_map/ppermute | solution.py:12
  177.1 0.7 copy-done.4
  177.8 2.8 multiply_convert_fusion.2
  180.6 3.0 %fusion.4 = f32[64,2048]{1,0:T(8,128)S(1)} fusion(bf16[64,768]{1,0:T(8,128)(2,1)S(1)} %get-tuple-element.25, bf16[2048,1,768]{2,0,1:T(8,128)(2,1)} %all-gather.8.cloned.1.call-done), kind=kOutput, calls=%fused_computation.9 | convolution fusion | flops 201326592 | bytes 3768320 | tf_op jit(solution)/shard_map/erf,def->erd/dot_general | solution.py:74
  183.6 1.1 fusion.28
  185.1 2.2 reduce.9
  187.4 0.9 reshape.364
  188.3 4.1 %all-to-all-start.3 = ((bf16[4,2,16384]{2,1,0:T(2,128)(2,1)}), bf16[4,2,16384]{2,1,0:T(2,128)(2,1)S(1)}, u32[]{:S(2)}, u32[]{:S(2)}) async-start(bf16[4,2,16384]{2,1,0:T(2,128)(2,1)} %reshape.364), calls=%async_computation.3 | async-start | bytes 524288 | tf_op jit(solution)/shard_map/all_to_all | solution.py:24
  192.4 2.2 copy.43
  194.6 11.6 %reduce.11 = bf16[2048,64]{1,0:T(8,128)(2,1)S(1)} reduce(bf16[2048,1,64]{2,1,0:T(2,128)(2,1)S(1)} %bitcast.160, bf16[]{:T(256)} %broadcast.146), dimensions={1}, to_apply=%bitcast.134.reduce_sub_computation | reduce | bytes 524290
  206.2 1.1 reshape.368
  207.3 15.4 %all-gather = bf16[512,768]{1,0:T(8,128)(2,1)S(1)} all-gather(bf16[64,768]{1,0:T(8,128)(2,1)S(1)} %copy-done.9), channel_id=2, replica_groups=mesh['dp'=8,'expert'=4] {'dp'}, dimensions={0}, use_global_device_ids=true | all-gather | bytes 884736 | tf_op jit(solution)/shard_map/all_gather | solution.py:88
  222.7 3.4 %all-to-all-start.5 = ((bf16[8,2,8192]{2,1,0:T(2,128)(2,1)}), bf16[8,2,8192]{2,1,0:T(2,128)(2,1)S(1)}, u32[]{:S(2)}, u32[]{:S(2)}) async-start(bf16[8,2,8192]{2,1,0:T(2,128)(2,1)} %reshape.368), calls=%async_computation.5 | async-start | bytes 524288 | tf_op jit(solution)/shard_map/all_to_all | solution.py:86
  226.1 20.0 %all-gather.1 = bf16[512,768]{1,0:T(8,128)(2,1)S(1)} all-gather(bf16[64,768]{1,0:T(8,128)(2,1)S(1)} %copy-done.7), channel_id=3, replica_groups=mesh['dp'=8,'expert'=4] {'dp'}, dimensions={0}, use_global_device_ids=true | all-gather | bytes 884736 | tf_op jit(solution)/shard_map/all_gather | solution.py:89
  246.9 1.7 copy.46
  248.6 3.6 %collective-permute-done.4 = bf16[1,64,768]{2,1,0:T(8,128)(2,1)S(1)} collective-permute-done((bf16[1,64,768]{2,1,0:T(8,128)(2,1)}, bf16[1,64,768]{2,1,0:T(8,128)(2,1)S(1)}, u32[]{:S(2)}, u32[]{:S(2)}) %collective-permute-start.4) | collective-permute-done | bytes 98336 | tf_op jit(solution)/shard_map/ppermute | solution.py:12
  252.6 1.7 copy.47
  254.6 4.5 %scatter_custom_fusion.1 = f32[768,2048]{1,0:T(8,128)} fusion(s32[64]{0:T(128)S(1)} %fusion.74, f32[]{:T(128)} %constant.67.clone.1, bf16[1,64,2048]{2,0,1:T(2,128)(2,1)S(1)} %bitcast.172), kind=kCustom, calls=%fused_computation.17 | custom fusion | flops 262144 | bytes 6815748 | tf_op jit(solution)/shard_map/scatter-add | solution.py:80
  259.1 4.9 %convert_element_type.75 = bf16[768,2048]{1,0:T(8,128)(2,1)} convert(f32[768,2048]{1,0:T(8,128)} %scatter_custom_fusion.1) | non-fusion elementwise | flops 1572864 | bytes 9437184 | tf_op jit(solution)/shard_map/convert_element_type | solution.py:81
  264.1 0.6 reshape.369
  264.7 0.6 copy.44
  265.8 1.2 convolution_add_fusion.6
  267.0 1.2 convolution_add_fusion.5
  268.2 1.2 convolution_add_fusion.4
  269.4 1.3 convolution_add_fusion.3
  271.0 1.2 convolution_add_fusion.1
  272.2 1.2 fusion.32
  273.4 3.0 %copy.48 = f32[256,1,768]{2,1,0:T(1,128)} copy(f32[256,1,768]{0,2,1:T(8,128)} %fusion.32) | data formatting | bytes 1572864
  (69 shorter events, 4.1 us)
Async XLA Ops:
  7.2 3.0 %copy-start = (bf16[768,2048]{1,0:T(8,128)(2,1)S(1)}, bf16[768,2048]{1,0:T(8,128)(2,1)}, u32[]{:S(2)}) copy-start(bf16[768,2048]{1,0:T(8,128)(2,1)} %param.8) | copy-start | bytes 9437188
  7.2 10.4 %copy-start.12 = (s32[1,4,1,16]{3,2,1,0:T(1,128)S(1)}, s32[1,4,1,16]{3,2,1,0:T(1,128)}, u32[]{:S(2)}) copy-start(s32[1,4,1,16]{3,2,1,0:T(1,128)} %param.10) | copy-start | bytes 772
  7.2 3.8 %copy-start.14 = (s32[1,4,1]{1,2,0:T(1,128)S(1)}, s32[1,4,1]{1,2,0:T(1,128)}, u32[]{:S(2)}) copy-start(s32[1,4,1]{1,2,0:T(1,128)} %param.11) | copy-start | bytes 52
  7.2 11.7 %copy-start.13 = (f32[1,4,1,16]{3,2,1,0:T(1,128)S(1)}, f32[1,4,1,16]{3,2,1,0:T(1,128)}, u32[]{:S(2)}) copy-start(f32[1,4,1,16]{3,2,1,0:T(1,128)} %param.12) | copy-start | bytes 772
  7.2 46.9 %all-gather.6.cloned.1.call-start = ((), (), s32[]{:S(2)}) async-start(), calls=%async_computation.6 | async-start | bytes 3538944 | tf_op jit(solution)/shard_map/all_gather | solution.py:41
  7.9 86.6 %all-gather.8.cloned.1.call-start = ((), (), s32[]{:S(2)}) async-start(), calls=%async_computation.7 | async-start | bytes 3538944 | tf_op jit(solution)/shard_map/all_gather | solution.py:42
  8.7 124.6 %all-gather.10.cloned.1.call-start = ((), (), s32[]{:S(2)}) async-start(), calls=%async_computation.8 | async-start | bytes 3538944 | tf_op jit(solution)/shard_map/all_gather | solution.py:43
  11.8 10.6 %all-to-all-start = ((bf16[4,16,2048]{2,1,0:T(8,128)(2,1)}), bf16[4,16,2048]{2,1,0:T(8,128)(2,1)S(1)}, u32[]{:S(2)}, u32[]{:S(2)}) async-start(bf16[4,16,2048]{2,1,0:T(8,128)(2,1)} %broadcast_multiply_fusion), calls=%async_computation | async-start | bytes 524288 | tf_op jit(solution)/shard_map/all_to_all | solution.py:20
  36.4 103.6 %all-to-all-start.4 = ((bf16[8,2,8192]{2,1,0:T(2,128)(2,1)}), bf16[8,2,8192]{2,1,0:T(2,128)(2,1)S(1)}, u32[]{:S(2)}, u32[]{:S(2)}) async-start(bf16[8,2,8192]{2,1,0:T(2,128)(2,1)} %reshape.366), calls=%async_computation.4 | async-start | bytes 524288 | tf_op jit(solution)/shard_map/all_to_all | solution.py:85
  56.6 76.7 %copy-start.5 = (f32[64,768]{1,0:T(8,128)}, f32[64,768]{1,0:T(8,128)S(1)}, u32[]{:S(2)}) copy-start(f32[64,768]{1,0:T(8,128)S(1)} %fusion.10) | copy-start | bytes 589828
  139.8 5.9 %collective-permute-start = (bf16[1,64,768]{2,1,0:T(8,128)(2,1)S(1)}, bf16[1,64,768]{2,1,0:T(8,128)(2,1)}, u32[]{:S(2)}, u32[]{:S(2)}) collective-permute-start(bf16[1,64,768]{2,1,0:T(8,128)(2,1)S(1)} %bitcast.186), channel_id=1, source_target_pairs={{0,4},{4,8},{8,12},{12,16},{16,20},{20,24},{24,28},{28,0},{1,5},{5... | collective-permute-start | bytes 294920 | tf_op jit(solution)/shard_map/ppermute | solution.py:12
  140.0 9.7 %all-to-all-start.1 = ((bf16[4,2,16384]{2,1,0:T(2,128)(2,1)}), bf16[4,2,16384]{2,1,0:T(2,128)(2,1)S(1)}, u32[]{:S(2)}, u32[]{:S(2)}) async-start(bf16[4,2,16384]{2,1,0:T(2,128)(2,1)} %reshape.362), calls=%async_computation.1 | async-start | bytes 524288 | tf_op jit(solution)/shard_map/all_to_all | solution.py:24
  145.7 25.1 %collective-permute-start.1 = (bf16[1,64,768]{2,1,0:T(8,128)(2,1)}, bf16[1,64,768]{2,1,0:T(8,128)(2,1)}, u32[]{:S(2)}, u32[]{:S(2)}) collective-permute-start(bf16[1,64,768]{2,1,0:T(8,128)(2,1)} %collective-permute-done), channel_id=1, source_target_pairs={{0,4},{4,8},{8,12},{12,16},{16,20},{20,24},{24,28},{28,0},{1,5},{5... | collective-permute-start | bytes 294920 | tf_op jit(solution)/shard_map/ppermute | solution.py:12
  150.7 5.3 %copy-start.3 = (bf16[768,2048]{1,0:T(8,128)(2,1)S(1)}, bf16[768,2048]{1,0:T(8,128)(2,1)}, u32[]{:S(2)}) copy-start(bf16[768,2048]{1,0:T(8,128)(2,1)} %param.9) | copy-start | bytes 9437188
  167.4 9.6 %all-to-all-start.2 = ((bf16[4,16,2048]{2,1,0:T(8,128)(2,1)}), bf16[4,16,2048]{2,1,0:T(8,128)(2,1)S(1)}, u32[]{:S(2)}, u32[]{:S(2)}) async-start(bf16[4,16,2048]{2,1,0:T(8,128)(2,1)} %multiply_convert_fusion), calls=%async_computation.2 | async-start | bytes 524288 | tf_op jit(solution)/shard_map/all_to_all | solution.py:20
  170.8 6.2 %collective-permute-start.2 = (bf16[1,64,768]{2,1,0:T(8,128)(2,1)}, bf16[1,64,768]{2,1,0:T(8,128)(2,1)}, u32[]{:S(2)}, u32[]{:S(2)}) collective-permute-start(bf16[1,64,768]{2,1,0:T(8,128)(2,1)} %collective-permute-done.1), channel_id=1, source_target_pairs={{0,4},{4,8},{8,12},{12,16},{16,20},{20,24},{24,28},{28,0},{1,5},{5... | collective-permute-start | bytes 294920 | tf_op jit(solution)/shard_map/ppermute | solution.py:12
  177.0 69.0 %collective-permute-start.3 = (bf16[1,64,768]{2,1,0:T(8,128)(2,1)}, bf16[1,64,768]{2,1,0:T(8,128)(2,1)}, u32[]{:S(2)}, u32[]{:S(2)}) collective-permute-start(bf16[1,64,768]{2,1,0:T(8,128)(2,1)} %collective-permute-done.2), channel_id=1, source_target_pairs={{0,4},{4,8},{8,12},{12,16},{16,20},{20,24},{24,28},{28,0},{1,5},{5... | collective-permute-start | bytes 294920 | tf_op jit(solution)/shard_map/ppermute | solution.py:12
  177.1 0.7 copy-start.4
  177.8 5.9 %copy-start.2 = (bf16[2048,1,768]{2,0,1:T(8,128)(2,1)S(1)}, bf16[2048,1,768]{2,0,1:T(8,128)(2,1)}, u32[]{:S(2)}) copy-start(bf16[2048,1,768]{2,0,1:T(8,128)(2,1)} %all-gather.6.cloned.1.call-done) | copy-start | bytes 9437188
  180.6 3.0 %copy-start.6 = (bf16[64,768]{1,0:T(8,128)(2,1)}, bf16[64,768]{1,0:T(8,128)(2,1)S(1)}, u32[]{:S(2)}) copy-start(bf16[64,768]{1,0:T(8,128)(2,1)S(1)} %get-tuple-element.25) | copy-start | bytes 294916
  180.6 4.1 %copy-start.8 = (bf16[64,768]{1,0:T(8,128)(2,1)}, bf16[64,768]{1,0:T(8,128)(2,1)S(1)}, u32[]{:S(2)}) copy-start(bf16[64,768]{1,0:T(8,128)(2,1)S(1)} %get-tuple-element.24) | copy-start | bytes 294916
  185.1 22.1 %copy-start.9 = (bf16[64,768]{1,0:T(8,128)(2,1)S(1)}, bf16[64,768]{1,0:T(8,128)(2,1)}, u32[]{:S(2)}) copy-start(bf16[64,768]{1,0:T(8,128)(2,1)} %copy-done.8) | copy-start | bytes 294916
  187.4 38.7 %copy-start.7 = (bf16[64,768]{1,0:T(8,128)(2,1)S(1)}, bf16[64,768]{1,0:T(8,128)(2,1)}, u32[]{:S(2)}) copy-start(bf16[64,768]{1,0:T(8,128)(2,1)} %copy-done.6) | copy-start | bytes 294916
  188.3 34.4 %all-to-all-start.3 = ((bf16[4,2,16384]{2,1,0:T(2,128)(2,1)}), bf16[4,2,16384]{2,1,0:T(2,128)(2,1)S(1)}, u32[]{:S(2)}, u32[]{:S(2)}) async-start(bf16[4,2,16384]{2,1,0:T(2,128)(2,1)} %reshape.364), calls=%async_computation.3 | async-start | bytes 524288 | tf_op jit(solution)/shard_map/all_to_all | solution.py:24
  222.7 41.4 %all-to-all-start.5 = ((bf16[8,2,8192]{2,1,0:T(2,128)(2,1)}), bf16[8,2,8192]{2,1,0:T(2,128)(2,1)S(1)}, u32[]{:S(2)}, u32[]{:S(2)}) async-start(bf16[8,2,8192]{2,1,0:T(2,128)(2,1)} %reshape.368), calls=%async_computation.5 | async-start | bytes 524288 | tf_op jit(solution)/shard_map/all_to_all | solution.py:86
  246.1 6.1 %collective-permute-start.4 = (bf16[1,64,768]{2,1,0:T(8,128)(2,1)}, bf16[1,64,768]{2,1,0:T(8,128)(2,1)S(1)}, u32[]{:S(2)}, u32[]{:S(2)}) collective-permute-start(bf16[1,64,768]{2,1,0:T(8,128)(2,1)} %collective-permute-done.3), channel_id=1, source_target_pairs={{0,4},{4,8},{8,12},{12,16},{16,20},{20,24},{24,28},{28,0},{1,5},{5... | collective-permute-start | bytes 294920 | tf_op jit(solution)/shard_map/ppermute | solution.py:12
  252.1 7.0 %copy-start.10 = (bf16[1,64,768]{2,1,0:T(8,128)(2,1)}, bf16[1,64,768]{2,1,0:T(8,128)(2,1)S(1)}, u32[]{:S(2)}) copy-start(bf16[1,64,768]{2,1,0:T(8,128)(2,1)S(1)} %collective-permute-done.4) | copy-start | bytes 294916
  252.1 11.9 %collective-permute-start.5 = (bf16[1,64,768]{2,1,0:T(8,128)(2,1)S(1)}, bf16[1,64,768]{2,1,0:T(8,128)(2,1)}, u32[]{:S(2)}, u32[]{:S(2)}) collective-permute-start(bf16[1,64,768]{2,1,0:T(8,128)(2,1)S(1)} %collective-permute-done.4), channel_id=1, source_target_pairs={{0,4},{4,8},{8,12},{12,16},{16,20},{20,24},{24,28},{28,0},{1,5},{5... | collective-permute-start | bytes 294920 | tf_op jit(solution)/shard_map/ppermute | solution.py:12
  264.1 8.2 %collective-permute-start.6 = (bf16[1,64,768]{2,1,0:T(8,128)(2,1)}, bf16[1,64,768]{2,1,0:T(8,128)(2,1)S(1)}, u32[]{:S(2)}, u32[]{:S(2)}) collective-permute-start(bf16[1,64,768]{2,1,0:T(8,128)(2,1)} %collective-permute-done.5), channel_id=1, source_target_pairs={{0,4},{4,8},{8,12},{12,16},{16,20},{20,24},{24,28},{28,0},{1,5},{5... | collective-permute-start | bytes 294920 | tf_op jit(solution)/shard_map/ppermute | solution.py:12
  265.8 5.0 %copy-start.11 = (bf16[1,64,768]{2,1,0:T(8,128)(2,1)S(1)}, bf16[1,64,768]{2,1,0:T(8,128)(2,1)}, u32[]{:S(2)}) copy-start(bf16[1,64,768]{2,1,0:T(8,128)(2,1)} %copy-done.10) | copy-start | bytes 294916
  269.4 7.1 %copy-start.1 = (bf16[768,2048]{1,0:T(8,128)(2,1)S(1)}, bf16[768,2048]{1,0:T(8,128)(2,1)}, u32[]{:S(2)}) copy-start(bf16[768,2048]{1,0:T(8,128)(2,1)} %param.8) | copy-start | bytes 9437188
Sparse Core Ops, SparseCore 0:
  9.7 44.3 all-gather.5
  55.7 38.7 all-gather.7
  96.2 37.1 all-gather.9
